TPU v7x, 32 devices: a whole 2x2x4 slice. The times are simulated.
32 devices in a mesh: group: 2 (over y), ctx: 4 (over z), head: 4 (over x, core).
Axes of the slice: x: 2, y: 2, z: 4, core: 2. Of those that a mesh axis runs over, the one named last changes fastest.
Arguments:
- query: bfloat16 [1024, 4096], P(('group', 'ctx'), 'head'), parts along dimension 0, may hold values from -8 to 8
- keys: bfloat16 [1024, 512], P(('group', 'ctx'), 'head'), parts along dimension 0, may hold values from -6 to 6
- values: bfloat16 [1024, 512], P(('group', 'ctx'), 'head'), parts along dimension 0, may hold values from -6 to 6
- residual: bfloat16 [1024, 2048], P(('group', 'ctx', 'head')), parts along dimension 0, may hold values from -15 to 15
- o_weight: bfloat16 [4096, 2048], P('head', 'ctx'), may hold values from -0.09375 to 0.09375
- gain: float32 [2048], replicated, may hold values from 0.1 to 1.9
- routes: int32 [1024, 8], P(('group', 'ctx', 'head')), parts along dimension 0, may hold values from 0 to 15, all different within a row; in each aligned block of 32 rows (0 to 31, 32 to 63, ...) at most 32 rows name the same one
- gates: float32 [1024, 8], P(('group', 'ctx', 'head')), parts along dimension 0, may hold values from 0.05 to 1
- w_gate: bfloat16 [16, 2048, 768], P(('ctx', 'head')), may hold values from -0.125 to 0.125
- w_up: bfloat16 [16, 2048, 768], P(('ctx', 'head')), may hold values from -0.125 to 0.125
- w_down: bfloat16 [16, 768, 2048], P(('ctx', 'head')), may hold values from -0.625 to 0.625
Outputs:
- mixed: bfloat16 [1024, 2048], P(('group', 'ctx', 'head')), parts along dimension 0
- expert_mix: bfloat16 [1024, 2048], P(('group', 'ctx', 'head')), parts along dimension 0
There are 2 independent parts, one for each index of `group`. A program takes and returns all parts, laid end to end along the dimension named above; an argument that names none is the same for every part. Nothing has to cross between parts.
Inputs may be any that keep to these rules, and one draw needn't show every extreme that they name: `routes`: the 8 experts of a token are distinct. In each aligned block of 32 tokens (the tokens of one owner device), no expert is named more than 32 times, a bound that some block reaches.
All inputs are finite; a program needn't handle non-finite values.
Results may differ from a plain program's by a relative error of at most 0.019.
Values may be sent and summed in bfloat16 or wider, within the bound.
No kernel may reach another device: no remote copies, remote signals or barrier semaphores. Data moves between devices by JAX's collectives and lax.ppermute only.
A program may use at most 128 MiB of HBM per device.

v0:
```python
import jax
import jax.numpy as jnp
from jax import lax
from jax.sharding import PartitionSpec as P

HEAD_DIMENSION = 128


def expert_apply(arrived, gate_proj, up_proj, down_proj):
    shape_in = arrived.shape
    flat_rows = arrived.reshape(-1, shape_in[-1])
    gate_act = jnp.dot(flat_rows, gate_proj, preferred_element_type=jnp.float32)
    up_act = jnp.dot(flat_rows, up_proj, preferred_element_type=jnp.float32)
    hidden = (jax.nn.silu(gate_act) * up_act).astype(jnp.bfloat16)
    output = jnp.dot(hidden, down_proj, preferred_element_type=jnp.float32).astype(jnp.bfloat16)
    return output.reshape(shape_in)


def body(query, keys, values, residual, o_weight, gain, routes, gates, w_gate, w_up, w_down):
    head_size = HEAD_DIMENSION
    query_rows = query.shape[0]
    kv_heads = keys.shape[1] // head_size
    q_heads = query.shape[1] // head_size
    head_replicas = q_heads // kv_heads
    scale = head_size ** (-0.5)
    queries = query.reshape(query_rows, kv_heads, head_replicas, head_size)
    first_pos = lax.axis_index("ctx") * query_rows
    query_pos = first_pos + jnp.arange(query_rows, dtype=jnp.int32)
    last_pos = first_pos + query_rows - 1

    def accumulate(carry, pieces):
        run_max, run_sum, run_acc = carry
        key_piece, value_piece = pieces
        width = key_piece.shape[0]
        key_pos = jnp.arange(width, dtype=jnp.int32)
        visible = key_pos[None, :] <= query_pos[:, None]
        scores = (
            jnp.einsum(
                "veqi,zei->eqvz",
                queries,
                key_piece.reshape(width, kv_heads, head_size),
                preferred_element_type=jnp.float32,
            )
            * scale
        )
        scores = jnp.where(visible, scores, -1e30)
        new_max = jnp.maximum(run_max, jnp.max(scores, axis=-1))
        weights = jnp.where(visible, jnp.exp(scores - new_max[..., None]), 0.0)
        new_sum = jnp.sum(weights, axis=-1)
        update = jnp.einsum(
            "pexa,apo->pexo",
            weights.astype(jnp.bfloat16),
            value_piece.reshape(width, kv_heads, head_size),
            preferred_element_type=jnp.float32,
        )
        return (new_max, new_sum, update)

    start_state = (
        jnp.full((kv_heads, head_replicas, query_rows), -1e30, jnp.float32),
        jnp.zeros((kv_heads, head_replicas, query_rows), jnp.float32),
        jnp.zeros((kv_heads, head_replicas, query_rows, head_size), jnp.float32),
    )
    pieces = (
        lax.all_gather(keys, "ctx", axis=0, tiled=True),
        lax.all_gather(values, "ctx", axis=0, tiled=True),
    )
    run_max, run_sum, run_acc = lax.cond(
        jnp.int32(0) > last_pos, lambda: start_state, lambda: accumulate(start_state, pieces)
    )
    attended = (
        (run_acc / run_sum[..., None])
        .transpose(2, 0, 1, 3)
        .reshape(query_rows, q_heads * head_size)
        .astype(jnp.bfloat16)
    )
    head_terms = jnp.dot(
        attended,
        lax.all_gather(o_weight, "ctx", axis=1, tiled=True),
        preferred_element_type=jnp.float32,
    )
    summed = lax.psum_scatter(
        head_terms.astype(jnp.bfloat16), "head", scatter_dimension=0, tiled=True
    ).astype(jnp.float32)
    mixed = (summed + residual.astype(jnp.float32)).astype(jnp.bfloat16)
    mixed_f = mixed.astype(jnp.float32)
    normed = (
        mixed_f * lax.rsqrt(jnp.mean(mixed_f * mixed_f, axis=-1, keepdims=True) + 1e-06) * gain
    ).astype(jnp.bfloat16)
    own_rows = residual.shape[0]
    model_dim = residual.shape[1]
    top_count = routes.shape[1]
    ctx_count = lax.axis_size("ctx")
    head_count = lax.axis_size("head")
    devices = ctx_count * head_count
    capacity = min(own_rows, max(2, 2 * own_rows * top_count // devices))
    expert_ids = routes.reshape(-1)
    onehot = (expert_ids[:, None] == jnp.arange(devices, dtype=jnp.int32)[None, :]).astype(
        jnp.int32
    )
    slots = jnp.sum((jnp.cumsum(onehot, axis=0) - 1) * onehot, axis=1)
    target = expert_ids * capacity + slots
    outgoing = (
        jnp.zeros((devices * capacity, model_dim), jnp.bfloat16)
        .at[target]
        .set(jnp.repeat(normed, top_count, axis=0))
    )
    outgoing = outgoing.reshape(devices, capacity, model_dim)
    gate_proj = w_gate[0]
    up_proj = w_up[0]
    down_proj = w_down[0]
    computed = expert_apply(
        lax.all_to_all(outgoing, ("ctx", "head"), split_axis=0, concat_axis=0, tiled=True),
        gate_proj,
        up_proj,
        down_proj,
    )
    returned = lax.all_to_all(computed, ("ctx", "head"), split_axis=0, concat_axis=0, tiled=True)
    selected_entries = returned.reshape(devices * capacity, model_dim)[target]
    selected_entries = selected_entries.astype(jnp.float32).reshape(own_rows, top_count, model_dim)
    weight_norm = gates / jnp.sum(gates, axis=-1, keepdims=True)
    expert_mix = jnp.sum(selected_entries * weight_norm[..., None], axis=1).astype(jnp.bfloat16)
    return (mixed, expert_mix)


def solution(mesh):
    return jax.shard_map(
        body,
        mesh=mesh,
        in_specs=(
            P(("group", "ctx"), "head"),
            P(("group", "ctx"), "head"),
            P(("group", "ctx"), "head"),
            P(("group", "ctx", "head"), None),
            P("head", "ctx"),
            P(),
            P(("group", "ctx", "head"), None),
            P(("group", "ctx", "head"), None),
            P(("ctx", "head"), None, None),
            P(("ctx", "head"), None, None),
            P(("ctx", "head"), None, None),
        ),
        out_specs=(P(("group", "ctx", "head"), None), P(("group", "ctx", "head"), None)),
        check_vma=False,
    )
```

profile of v0, /device:TPU:11, one launch (start us, length us, event | category | flops | bytes accessed | tf_op | source)
XLA Modules:
  0.0 255.7 jit_solution(5889170970731669494)
XLA Ops:
  7.2 0.7 all-gather.2.cloned.1.call-update
  8.0 11.0 %all_gather.10 = bf16[512,128]{1,0:T(8,128)(2,1)S(1)} all-gather(bf16[128,128]{1,0:T(8,128)(2,1)} %param.15), channel_id=1, replica_groups=mesh['group'=2,'ctx'=4,'head'=4] {'ctx'}, dimensions={0}, use_global_device_ids=true | all-gather | bytes 163840 | tf_op jit(solution)/shard_map/all_gather | solution.py:65
  19.0 14.5 %all_gather.9 = bf16[512,128]{1,0:T(8,128)(2,1)S(1)} all-gather(bf16[128,128]{1,0:T(8,128)(2,1)} %param.14), channel_id=1, replica_groups=mesh['group'=2,'ctx'=4,'head'=4] {'ctx'}, dimensions={0}, use_global_device_ids=true | all-gather | bytes 163840 | tf_op jit(solution)/shard_map/all_gather | solution.py:64
  33.5 2.6 %conditional.1 = (f32[1,8,128]{2,1,0:T(8,128)S(1)}, f32[1,8,128,128]{2,3,1,0:T(8,128)S(1)}) conditional(s32[]{:T(128)} %convert_element_type.54, (s32[]{:T(128)}, s32[128]{0:T(128)S(1)}, bf16[128,1024]{1,0:T(8,128)(2,1)}, bf16[512,128]{1,0:T(8,128)(2,1)S(1)}, bf16[512,128]{1,0:T(8,128)(2,1)S(1)}) %tuple.16, () %tuple.17), branch_computations={%region_0.3_spmd, %region_3.4_spmd} | conditional | flops 275315840 | bytes 7628308 | solution.py:67
  33.5 0.1 iota_compare_fusion
  33.6 1.4 fusion
  35.0 0.6 convolution_bitcast_fusion
  35.6 0.5 fusion.2
  36.2 0.1 divide_convert_fusion
  36.2 55.0 %all-gather.2.cloned.1.call-done = bf16[1024,2048]{1,0:T(8,128)(2,1)} async-done(((bf16[1024,512]{1,0:T(8,128)(2,1)}), bf16[1024,2048]{1,0:T(8,128)(2,1)}) %all-gather.2.cloned.1.call-update) | async-done | bytes 4194320 | tf_op jit(solution)/shard_map/all_gather | solution.py:78
  91.2 3.8 %convolution_convert_fusion = bf16[128,2048]{1,0:T(8,128)(2,1)} fusion(bf16[128,1024]{0,1:T(8,128)(2,1)S(1)} %bitcast.93, bf16[1024,2048]{1,0:T(8,128)(2,1)} %all-gather.2.cloned.1.call-done), kind=kOutput, calls=%fused_computation.32 | convolution fusion | flops 537133056 | bytes 4980736 | tf_op jit(solution)/shard_map/dot_general | solution.py:76
  95.0 0.1 copy.21
  95.1 0.1 eq.29
  95.2 0.1 eq.25
  95.3 0.6 reduce-window.6
  95.9 0.2 slice_reduce_fusion
  96.1 0.1 copy.20
  96.2 0.1 mul.68
  96.3 0.1 fusion.40
  96.4 20.1 %reduce-scatter.2.cloned.1.call-done = bf16[32,2048]{1,0:T(8,128)(2,1)} async-done(((bf16[128,2048]{1,0:T(8,128)(2,1)}), bf16[32,2048]{1,0:T(8,128)(2,1)}) %reduce-scatter.2.cloned.1.call-update) | async-done | bytes 131088 | tf_op jit(solution)/shard_map/reduce_scatter | solution.py:81
  116.5 1.1 fusion.36
  117.6 0.1 fusion.38
  117.7 3.7 %scatter_custom_fusion = bf16[512,2048]{1,0:T(8,128)(2,1)} fusion(s32[256]{0:T(256)S(1)} %bitcast.96, bf16[]{:T(256)} %constant.28.clone.1, bf16[32,2048]{1,0:T(8,128)(2,1)S(1)} %fusion.38), kind=kCustom, calls=%fused_computation.36 | custom fusion | bytes 2228226 | tf_op jit(solution)/shard_map/scatter | solution.py:105
  121.5 54.1 %all_to_all.10 = bf16[16,32,2048]{2,1,0:T(8,128)(2,1)S(1)} all-to-all(bf16[16,32,2048]{2,1,0:T(8,128)(2,1)} %bitcast.89), channel_id=1, replica_groups=mesh['group'=2,'ctx'=4,'head'=4] {'ctx','head'}, dimensions={0} | all-to-all | bytes 4194304 | tf_op jit(solution)/shard_map/all_to_all | solution.py:112
  175.5 1.3 copy-done.1
  176.8 3.0 %fusion.22 = f32[512,768]{1,0:T(8,128)} fusion(bf16[512,2048]{1,0:T(8,128)(2,1)S(1)} %bitcast.91, bf16[1,2048,768]{2,1,0:T(8,128)(2,1)S(1)} %copy-done.7), kind=kOutput, calls=%fused_computation.29 | convolution fusion | flops 1610612736 | bytes 6815744 | tf_op jit(solution)/shard_map/dot_general | solution.py:12
  179.8 8.3 %fusion.24 = bf16[512,2048]{1,0:T(8,128)(2,1)} fusion(bf16[1,768,2048]{2,1,0:T(8,128)(2,1)S(1)} %copy-done, f32[512,768]{1,0:T(8,128)} %fusion.22, bf16[512,2048]{1,0:T(8,128)(2,1)} %bitcast.92, bf16[1,2048,768]{2,1,0:T(8,128)(2,1)} %param.22), kind=kOutput, calls=%fused_computation.31 | convolution fusion | flops 3224633344 | bytes 12058624 | tf_op jit(solution)/shard_map/dot_general | solution.py:15
  188.1 5.2 %all-to-all-start.1 = ((bf16[16,32,2048]{2,1,0:T(8,128)(2,1)}), bf16[16,32,2048]{2,1,0:T(8,128)(2,1)}, u32[]{:S(2)}, u32[]{:S(2)}) async-start(bf16[16,32,2048]{2,1,0:T(8,128)(2,1)} %bitcast.90), calls=%async_computation.2 | async-start | bytes 4194304 | tf_op jit(solution)/shard_map/all_to_all | solution.py:117
  193.3 0.1 copy.24
  193.4 47.4 %all-to-all-done.1 = bf16[16,32,2048]{2,1,0:T(8,128)(2,1)} async-done(((bf16[16,32,2048]{2,1,0:T(8,128)(2,1)}), bf16[16,32,2048]{2,1,0:T(8,128)(2,1)}, u32[]{:S(2)}, u32[]{:S(2)}) %all-to-all-start.1) | async-done | bytes 2097184 | tf_op jit(solution)/shard_map/all_to_all | solution.py:117
  240.8 5.2 %gather_fusion = bf16[256,2048]{1,0:T(8,128)(2,1)} fusion(bf16[512,2048]{1,0:T(8,128)(2,1)} %bitcast.20, s32[1024]{0:T(1024)S(1)} %pad_clamp_fusion), kind=kCustom, calls=%fused_computation | custom fusion | bytes 2098176 | tf_op jit(solution)/shard_map/gather | solution.py:118
  246.0 2.9 %fusion.27 = bf16[32,2048]{1,0:T(8,128)(2,1)} fusion(bf16[256,2048]{1,0:T(8,128)(2,1)} %gather_fusion, f32[32,8]{1,0:T(8,128)S(1)} %copy.24), kind=kLoop, calls=%fused_computation.34 | loop fusion | flops 1507328 | bytes 1180672 | tf_op jit(solution)/shard_map/reduce_sum | solution.py:121
  (30 shorter events, 0.2 us)
Async XLA Ops:
  7.2 172.6 %copy-start = (bf16[1,768,2048]{2,1,0:T(8,128)(2,1)S(1)}, bf16[1,768,2048]{2,1,0:T(8,128)(2,1)}, u32[]{:S(2)}) copy-start(bf16[1,768,2048]{2,1,0:T(8,128)(2,1)} %param.23) | copy-start | bytes 9437188
  7.2 84.0 %all-gather.2.cloned.1.call-start = ((), (), s32[]{:S(2)}) async-start(), calls=%async_computation.3 | async-start | bytes 5242880 | tf_op jit(solution)/shard_map/all_gather | solution.py:78
  7.9 108.6 %reduce-scatter.2.cloned.1.call-start = ((), (), s32[]{:S(2)}) async-start(), calls=%async_computation.4 | async-start | bytes 655360 | tf_op jit(solution)/shard_map/reduce_scatter | solution.py:81
  91.2 3.8 %copy-start.4 = (s32[32,8]{0,1:T(8,128)S(1)}, s32[32,8]{0,1:T(8,128)}, u32[]{:S(2)}) copy-start(s32[32,8]{0,1:T(8,128)} %param.19) | copy-start | bytes 3076
  91.2 25.3 %copy-start.3 = (bf16[32,2048]{1,0:T(8,128)(2,1)S(1)}, bf16[32,2048]{1,0:T(8,128)(2,1)}, u32[]{:S(2)}) copy-start(bf16[32,2048]{1,0:T(8,128)(2,1)} %param.16) | copy-start | bytes 393220
  91.2 26.4 %copy-start.6 = (f32[2048]{0:T(1024)S(1)}, f32[2048]{0:T(1024)}, u32[]{:S(2)}) copy-start(f32[2048]{0:T(1024)} %param.18) | copy-start | bytes 24580
  117.6 58.0 %copy-start.2 = (bf16[32,2048]{1,0:T(8,128)(2,1)}, bf16[32,2048]{1,0:T(8,128)(2,1)S(1)}, u32[]{:S(2)}) copy-start(bf16[32,2048]{1,0:T(8,128)(2,1)S(1)} %get-tuple-element.28) | copy-start | bytes 393220
  121.5 55.4 %copy-start.7 = (bf16[1,2048,768]{2,1,0:T(8,128)(2,1)S(1)}, bf16[1,2048,768]{2,1,0:T(8,128)(2,1)}, u32[]{:S(2)}) copy-start(bf16[1,2048,768]{2,1,0:T(8,128)(2,1)} %param.21) | copy-start | bytes 9437188
  175.5 1.3 copy-start.1
  188.1 5.2 %copy-start.5 = (f32[32,8]{0,1:T(8,128)S(1)}, f32[32,8]{0,1:T(8,128)}, u32[]{:S(2)}) copy-start(f32[32,8]{0,1:T(8,128)} %param.20) | copy-start | bytes 3076
  188.1 52.7 %all-to-all-start.1 = ((bf16[16,32,2048]{2,1,0:T(8,128)(2,1)}), bf16[16,32,2048]{2,1,0:T(8,128)(2,1)}, u32[]{:S(2)}, u32[]{:S(2)}) async-start(bf16[16,32,2048]{2,1,0:T(8,128)(2,1)} %bitcast.90), calls=%async_computation.2 | async-start | bytes 4194304 | tf_op jit(solution)/shard_map/all_to_all | solution.py:117
Sparse Core Ops, SparseCore 0:
  9.6 81.6 all-gather.1
  95.1 21.3 reduce-scatter.1
where the time goes:
time: 256 us
  waiting for transfers between devices  123 us (48%)
  blocking collectives  79.6 us (31%)
  matrix products  17.1 us (7%)
  between operations  14.1 us (6%)
  local copies, waits for them, and re-layouts  11 us (4%)
  other arithmetic  5.41 us (2%)
  starting transfers between devices  5.23 us (2%)
    all_gather x1, waiting for transfers between devices, body(): lax.all_gather(o_weight, 'ctx', axis=1, tiled=True)  55 us
    all_to_all x1, blocking collectives, body(): lax.all_to_all(outgoing, ('ctx', 'head'), split_axis=0, concat_axis=0, ti...  54.1 us
    all_to_all x1, waiting for transfers between devices, body(): lax.all_to_all(computed, ('ctx', 'head'), split_axis=0, concat_axis=0, ti...  47.4 us
    reduce_scatter x1, waiting for transfers between devices, body(): lax.psum_scatter(head_terms.astype(jnp.bfloat16), 'head', scatter_dimensi...  20.1 us
    all_gather x1, blocking collectives, body(): lax.all_gather(keys, 'ctx', axis=0, tiled=True)  14.5 us
    all_gather x1, blocking collectives, body(): lax.all_gather(values, 'ctx', axis=0, tiled=True)  11 us
    dot_general x1, matrix products, expert_apply(): jnp.dot(hidden, down_proj, preferred_element_type=jnp.float32)  8.28 us
    gather x1, local copies, waits for them, and re-layouts, body(): selected_entries = returned.reshape(devices * capacity, model_dim)[target]  5.21 us
  transfers between devices with their start and end apart: 3, of which 3 were waited for; matrix products, arithmetic and copies ran while one was open for 2% of the time, Pallas kernels for 0%

commit v1 on v0

--- a/solution.py
+++ b/solution.py
@@ -4,6 +4,29 @@
 from jax.sharding import PartitionSpec as P
 
 HEAD_DIMENSION = 128
+
+
+def _write_tiles(xx, row_dim, work_x):
+    mixed_arr, moved = (xx.shape[:row_dim], xx.shape[row_dim + 1 :])
+    return jnp.moveaxis(xx.reshape(*mixed_arr, work_x, -1, *moved), row_dim, 0)
+
+
+def state_limits_on(view, array_dim):
+    part_next = list(view.shape[1:])
+    part_next[array_dim] *= view.shape[0]
+    return jnp.moveaxis(view, 0, array_dim).reshape(part_next)
+
+
+def guide_state(z_in, a_name, inner_x, state=0):
+    heard, z = (lax.axis_size(a_name), lax.axis_index(a_name))
+    v_next = _write_tiles(z_in, inner_x, heard)
+    current_arr = v_next
+    for w in range(1, heard):
+        t1, a_now = ((z + w) % heard, (z - w) % heard)
+        local_next = lax.dynamic_index_in_dim(v_next, t1, 0)
+        ready = lax.ppermute(local_next, a_name, [(t, (t + w) % heard) for t in range(heard)])
+        current_arr = lax.dynamic_update_slice_in_dim(current_arr, ready, a_now, axis=0)
+    return state_limits_on(current_arr, state)
 
 
 def expert_apply(arrived, gate_proj, up_proj, down_proj):
@@ -114,7 +137,7 @@
         up_proj,
         down_proj,
     )
-    returned = lax.all_to_all(computed, ("ctx", "head"), split_axis=0, concat_axis=0, tiled=True)
+    returned = guide_state(computed, ("ctx", "head"), 0)
     selected_entries = returned.reshape(devices * capacity, model_dim)[target]
     selected_entries = selected_entries.astype(jnp.float32).reshape(own_rows, top_count, model_dim)
     weight_norm = gates / jnp.sum(gates, axis=-1, keepdims=True)

time: 256 us -> 269 us (1.051)
  blocking collectives: 79.6 us -> 25.5 us
  waiting for transfers between devices: 123 us -> 148 us
  starting transfers between devices: 5.23 us -> 27.8 us
  local copies, waits for them, and re-layouts: 11 us -> 24.2 us
    all_to_all x1 -> x0, blocking collectives: 54.1 us -> none  [body(): lax.all_to_all(outgoing, ('ctx', 'head'), split_axis=0, concat_axis=0, ti...]
    ppermute x0 -> x15, waiting for transfers between devices: none -> 24.3 us  [guide_state(): lax.ppermute(local_next, a_name, [(t, (t + w) % heard) for t in range(hea...]
    ppermute x0 -> x15, starting transfers between devices: none -> 21.2 us  [guide_state(): lax.ppermute(local_next, a_name, [(t, (t + w) % heard) for t in range(hea...]
    dynamic_update_slice x0 -> x14, local copies, waits for them, and re-layouts: none -> 10.1 us  [guide_state(): lax.dynamic_update_slice_in_dim(current_arr, ready, a_now, axis=0)]
    dynamic_slice x0 -> x2, local copies, waits for them, and re-layouts: none -> 3.6 us  [guide_state(): local_next = lax.dynamic_index_in_dim(v_next, t1, 0)]
  transfers between devices with their start and end apart: 3 -> 18, of which waited for: 3 -> 9; matrix products, arithmetic and copies ran while one was open for 2% -> 6% of each run, Pallas kernels for 0% -> 0%
where the time goes in v1:
time: 269 us; the launch traced here: 266 us
  waiting for transfers between devices  148 us (55%)
  starting transfers between devices  27.8 us (10%)
  blocking collectives  25.5 us (9%)
  local copies, waits for them, and re-layouts  24.2 us (9%)
  matrix products  19.6 us (7%)
  between operations  14.2 us (5%)
  other arithmetic  7.26 us (3%)
    all_gather x1, waiting for transfers between devices, body(): lax.all_gather(o_weight, 'ctx', axis=1, tiled=True)  55 us
    all_to_all x1, waiting for transfers between devices, body(): lax.all_to_all(outgoing, ('ctx', 'head'), split_axis=0, concat_axis=0, ti...  47.5 us
    ppermute x15, waiting for transfers between devices, guide_state(): lax.ppermute(local_next, a_name, [(t, (t + w) % heard) for t in range(hea...  24.3 us
    ppermute x15, starting transfers between devices, guide_state(): lax.ppermute(local_next, a_name, [(t, (t + w) % heard) for t in range(hea...  21.2 us
    reduce_scatter x1, waiting for transfers between devices, body(): lax.psum_scatter(head_terms.astype(jnp.bfloat16), 'head', scatter_dimensi...  20.1 us
    all_gather x1, blocking collectives, body(): lax.all_gather(keys, 'ctx', axis=0, tiled=True)  14.5 us
    all_gather x1, blocking collectives, body(): lax.all_gather(values, 'ctx', axis=0, tiled=True)  11 us
    dynamic_update_slice x14, local copies, waits for them, and re-layouts, guide_state(): lax.dynamic_update_slice_in_dim(current_arr, ready, a_now, axis=0)  10.1 us
  transfers between devices with their start and end apart: 18, of which 9 were waited for; matrix products, arithmetic and copies ran while one was open for 6% of the time, Pallas kernels for 0%

profile of v1, /device:TPU:11, one launch (start us, length us, event | category | flops | bytes accessed | tf_op | source)
XLA Modules:
  0.0 266.2 jit_solution(3816744185799500039)
XLA Ops:
  8.0 11.0 %all_gather.10 = bf16[512,128]{1,0:T(8,128)(2,1)S(1)} all-gather(bf16[128,128]{1,0:T(8,128)(2,1)} %param.15), channel_id=1, replica_groups=mesh['group'=2,'ctx'=4,'head'=4] {'ctx'}, dimensions={0}, use_global_device_ids=true | all-gather | bytes 163840 | tf_op jit(solution)/shard_map/all_gather | solution.py:88
  19.0 14.5 %all_gather.9 = bf16[512,128]{1,0:T(8,128)(2,1)S(1)} all-gather(bf16[128,128]{1,0:T(8,128)(2,1)} %param.14), channel_id=1, replica_groups=mesh['group'=2,'ctx'=4,'head'=4] {'ctx'}, dimensions={0}, use_global_device_ids=true | all-gather | bytes 163840 | tf_op jit(solution)/shard_map/all_gather | solution.py:87
  33.5 2.6 conditional.1
  33.6 1.4 fusion
  36.2 55.0 %all-gather.2.cloned.1.call-done = bf16[1024,2048]{1,0:T(8,128)(2,1)} async-done(((bf16[1024,512]{1,0:T(8,128)(2,1)}), bf16[1024,2048]{1,0:T(8,128)(2,1)}) %all-gather.2.cloned.1.call-update) | async-done | bytes 4194320 | tf_op jit(solution)/shard_map/all_gather | solution.py:101
  91.2 3.8 %convolution_convert_fusion = bf16[128,2048]{1,0:T(8,128)(2,1)} fusion(bf16[128,1024]{0,1:T(8,128)(2,1)S(1)} %bitcast.93, bf16[1024,2048]{1,0:T(8,128)(2,1)} %all-gather.2.cloned.1.call-done), kind=kOutput, calls=%fused_computation.32 | convolution fusion | flops 537133056 | bytes 4980736 | tf_op jit(solution)/shard_map/dot_general | solution.py:99
  96.4 20.1 %reduce-scatter.2.cloned.1.call-done = bf16[32,2048]{1,0:T(8,128)(2,1)} async-done(((bf16[128,2048]{1,0:T(8,128)(2,1)}), bf16[32,2048]{1,0:T(8,128)(2,1)}) %reduce-scatter.2.cloned.1.call-update) | async-done | bytes 131088 | tf_op jit(solution)/shard_map/reduce_scatter | solution.py:104
  117.8 3.7 %scatter_custom_fusion = bf16[512,2048]{1,0:T(8,128)(2,1)} fusion(s32[256]{0:T(256)S(1)} %bitcast.96, bf16[]{:T(256)} %constant.230.clone.1, bf16[32,2048]{1,0:T(8,128)(2,1)S(1)} %fusion.38), kind=kCustom, calls=%fused_computation.36 | custom fusion | bytes 2228226 | tf_op jit(solution)/shard_map/scatter | solution.py:128
  121.5 6.5 %all-to-all-start = ((bf16[16,32,2048]{2,1,0:T(8,128)(2,1)}), bf16[16,32,2048]{2,1,0:T(8,128)(2,1)}, u32[]{:S(2)}, u32[]{:S(2)}) async-start(bf16[16,32,2048]{2,1,0:T(8,128)(2,1)} %bitcast.92), calls=%async_computation.1 | async-start | bytes 4194304 | tf_op jit(solution)/shard_map/all_to_all | solution.py:135
  128.0 47.5 %all-to-all-done = bf16[16,32,2048]{2,1,0:T(8,128)(2,1)} async-done(((bf16[16,32,2048]{2,1,0:T(8,128)(2,1)}), bf16[16,32,2048]{2,1,0:T(8,128)(2,1)}, u32[]{:S(2)}, u32[]{:S(2)}) %all-to-all-start) | async-done | bytes 2097184 | tf_op jit(solution)/shard_map/all_to_all | solution.py:135
  175.5 5.5 %fusion.22 = f32[512,768]{1,0:T(8,128)} fusion(bf16[512,2048]{1,0:T(8,128)(2,1)} %bitcast.15, bf16[1,2048,768]{2,1,0:T(8,128)(2,1)} %param.21), kind=kOutput, calls=%fused_computation.29 | convolution fusion | flops 1610612736 | bytes 6815744 | tf_op jit(solution)/shard_map/dot_general | solution.py:35
  181.0 8.3 %fusion.24 = bf16[512,2048]{1,0:T(8,128)(2,1)} fusion(bf16[1,768,2048]{2,1,0:T(8,128)(2,1)S(1)} %copy-done, f32[512,768]{1,0:T(8,128)} %fusion.22, bf16[512,2048]{1,0:T(8,128)(2,1)} %bitcast.15, bf16[1,2048,768]{2,1,0:T(8,128)(2,1)} %param.22), kind=kOutput, calls=%fused_computation.31 | convolution fusion | flops 3224633344 | bytes 12058624 | tf_op jit(solution)/shard_map/dot_general | solution.py:38
  190.2 1.7 collective-permute-start
  191.9 1.9 collective-permute-done
  193.9 2.7 %constant_dynamic-slice_fusion = (bf16[1,1,32,2048]{3,2,0,1:T(8,128)(2,1)S(1)}, bf16[1,1,32,2048]{3,2,0,1:T(8,128)(2,1)S(1)}, bf16[1,1,32,2048]{3,2,0,1:T(8,128)...) fusion(bf16[16,1,32,2048]{3,2,0,1:T(8,128)(2,1)} %bitcast.90, ...), kind=kLoop, calls=%fused_computation.56 | loop fusion | bytes 3932220 | tf_op jit(solution)/shard_map/jit(dynamic_index_in_dim)/dynamic_slice | solution.py:26
  197.9 1.3 pad_clamp_fusion
  199.2 1.1 collective-permute-start.2
  200.3 4.2 %collective-permute-start.3 = (bf16[1,1,32,2048]{3,2,0,1:T(8,128)(2,1)}, bf16[1,1,32,2048]{3,2,0,1:T(8,128)(2,1)S(1)}, u32[]{:S(2)}, u32[]{:S(2)}) collective-permute-start(bf16[1,1,32,2048]{3,2,0,1:T(8,128)(2,1)} %get-tuple-element.42), channel_id=1, source_target_pairs={{0,4},{1,5},{2,6},{3,7},{4,8},{5,9},{6,10},{7,11},{8,12},{9,13},{1... | collective-permute-start | bytes 393224 | tf_op jit(solution)/shard_map/ppermute | solution.py:27
  204.5 3.2 %collective-permute-start.5 = (bf16[1,1,32,2048]{3,2,0,1:T(8,128)(2,1)}, bf16[1,1,32,2048]{3,2,0,1:T(8,128)(2,1)S(1)}, u32[]{:S(2)}, u32[]{:S(2)}) collective-permute-start(bf16[1,1,32,2048]{3,2,0,1:T(8,128)(2,1)} %get-tuple-element.40), channel_id=1, source_target_pairs={{0,6},{1,7},{2,8},{3,9},{4,10},{5,11},{6,12},{7,13},{8,14},{9,15},... | collective-permute-start | bytes 393224 | tf_op jit(solution)/shard_map/ppermute | solution.py:27
  207.7 1.6 constant_dynamic-update-slice_fusion.13
  209.2 1.5 collective-permute-start.7
  211.4 1.8 collective-permute-start.8
  213.9 1.7 collective-permute-start.9
  216.2 13.0 %collective-permute-done.5 = bf16[1,1,32,2048]{3,2,0,1:T(8,128)(2,1)S(1)} collective-permute-done((bf16[1,1,32,2048]{3,2,0,1:T(8,128)(2,1)}, bf16[1,1,32,2048]{3,2,0,1:T(8,128)(2,1)S(1)}, u32[]{:S(2)}, u32[]{:S(2)}) %collective-permute-start.5) | collective-permute-done | bytes 131104 | tf_op jit(solution)/shard_map/ppermute | solution.py:27
  229.2 3.5 %collective-permute-start.10 = (bf16[1,1,32,2048]{3,2,0,1:T(8,128)(2,1)}, bf16[1,1,32,2048]{3,2,0,1:T(8,128)(2,1)S(1)}, u32[]{:S(2)}, u32[]{:S(2)}) collective-permute-start(bf16[1,1,32,2048]{3,2,0,1:T(8,128)(2,1)} %get-tuple-element.35), channel_id=1, source_target_pairs={{0,11},{1,12},{2,13},{3,14},{4,15},{5,0},{6,1},{7,2},{8,3},{9,4},{... | collective-permute-start | bytes 393224 | tf_op jit(solution)/shard_map/ppermute | solution.py:27
  233.3 1.3 collective-permute-done.6
  235.3 3.7 %collective-permute-done.7 = bf16[1,1,32,2048]{3,2,0,1:T(8,128)(2,1)S(1)} collective-permute-done((bf16[1,1,32,2048]{3,2,0,1:T(8,128)(2,1)}, bf16[1,1,32,2048]{3,2,0,1:T(8,128)(2,1)S(1)}, u32[]{:S(2)}, u32[]{:S(2)}) %collective-permute-start.7) | collective-permute-done | bytes 131104 | tf_op jit(solution)/shard_map/ppermute | solution.py:27
  239.7 2.4 collective-permute-start.13
  244.1 1.4 collective-permute-done.11
  246.9 3.0 %collective-permute-done.13 = bf16[1,1,32,2048]{3,2,0,1:T(8,128)(2,1)S(1)} collective-permute-done((bf16[1,1,32,2048]{3,2,0,1:T(8,128)(2,1)S(1)}, bf16[1,1,32,2048]{3,2,0,1:T(8,128)(2,1)S(1)}, u32[]{:S(2)}, u32[]{:S(2)}) %collective-permute-start.13) | collective-permute-done | bytes 131104 | tf_op jit(solution)/shard_map/ppermute | solution.py:27
  251.1 5.4 %gather_fusion = bf16[256,2048]{1,0:T(8,128)(2,1)} fusion(bf16[512,2048]{1,0:T(8,128)(2,1)} %bitcast.91, s32[1024]{0:T(1024)} %pad_clamp_fusion), kind=kCustom, calls=%fused_computation | custom fusion | bytes 2098176 | tf_op jit(solution)/shard_map/gather | solution.py:141
  256.5 2.9 %fusion.27 = bf16[32,2048]{1,0:T(8,128)(2,1)} fusion(bf16[256,2048]{1,0:T(8,128)(2,1)} %gather_fusion, f32[32,8]{1,0:T(8,128)S(1)} %copy.24), kind=kLoop, calls=%fused_computation.34 | loop fusion | flops 1507328 | bytes 1180672 | tf_op jit(solution)/shard_map/reduce_sum | solution.py:144
  (73 shorter events, 15.5 us)
Async XLA Ops:
  7.2 173.8 %copy-start = (bf16[1,768,2048]{2,1,0:T(8,128)(2,1)S(1)}, bf16[1,768,2048]{2,1,0:T(8,128)(2,1)}, u32[]{:S(2)}) copy-start(bf16[1,768,2048]{2,1,0:T(8,128)(2,1)} %param.23) | copy-start | bytes 9437188
  7.2 84.0 %all-gather.2.cloned.1.call-start = ((), (), s32[]{:S(2)}) async-start(), calls=%async_computation.2 | async-start | bytes 5242880 | tf_op jit(solution)/shard_map/all_gather | solution.py:101
  7.9 108.6 %reduce-scatter.2.cloned.1.call-start = ((), (), s32[]{:S(2)}) async-start(), calls=%async_computation.3 | async-start | bytes 655360 | tf_op jit(solution)/shard_map/reduce_scatter | solution.py:104
  91.2 3.8 %copy-start.3 = (s32[32,8]{0,1:T(8,128)S(1)}, s32[32,8]{0,1:T(8,128)}, u32[]{:S(2)}) copy-start(s32[32,8]{0,1:T(8,128)} %param.19) | copy-start | bytes 3076
  91.2 25.3 %copy-start.2 = (bf16[32,2048]{1,0:T(8,128)(2,1)S(1)}, bf16[32,2048]{1,0:T(8,128)(2,1)}, u32[]{:S(2)}) copy-start(bf16[32,2048]{1,0:T(8,128)(2,1)} %param.16) | copy-start | bytes 393220
  91.2 26.4 %copy-start.5 = (f32[2048]{0:T(1024)S(1)}, f32[2048]{0:T(1024)}, u32[]{:S(2)}) copy-start(f32[2048]{0:T(1024)} %param.18) | copy-start | bytes 24580
  96.4 25.1 %copy-start.6 = (s32[256,1]{0,1:T(1,128)}, s32[256,1]{0,1:T(1,128)S(1)}, u32[]{:S(2)}) copy-start(s32[256,1]{0,1:T(1,128)S(1)} %compare_select_fusion) | copy-start | bytes 3076
  117.6 3.9 %copy-start.1 = (bf16[32,2048]{1,0:T(8,128)(2,1)}, bf16[32,2048]{1,0:T(8,128)(2,1)S(1)}, u32[]{:S(2)}) copy-start(bf16[32,2048]{1,0:T(8,128)(2,1)S(1)} %get-tuple-element.28) | copy-start | bytes 393220
  121.5 54.0 %all-to-all-start = ((bf16[16,32,2048]{2,1,0:T(8,128)(2,1)}), bf16[16,32,2048]{2,1,0:T(8,128)(2,1)}, u32[]{:S(2)}, u32[]{:S(2)}) async-start(bf16[16,32,2048]{2,1,0:T(8,128)(2,1)} %bitcast.92), calls=%async_computation.1 | async-start | bytes 4194304 | tf_op jit(solution)/shard_map/all_to_all | solution.py:135
  181.0 10.9 %copy-start.4 = (f32[32,8]{0,1:T(8,128)S(1)}, f32[32,8]{0,1:T(8,128)}, u32[]{:S(2)}) copy-start(f32[32,8]{0,1:T(8,128)} %param.20) | copy-start | bytes 3076
  190.2 3.7 %collective-permute-start = (bf16[1,1,32,2048]{3,2,0,1:T(8,128)(2,1)S(1)}, bf16[1,1,32,2048]{3,2,0,1:T(8,128)(2,1)}, u32[]{:S(2)}, u32[]{:S(2)}) collective-permute-start(bf16[1,1,32,2048]{3,2,0,1:T(8,128)(2,1)S(1)} %constant_dynamic-slice_fusion.14), channel_id=1, source_target_pairs={{0,1},{1,2},{2,3},{3,4},{4,5},{5,6},{6,7},{7,8},{8,9},{9,10},{10,1... | collective-permute-start | bytes 393224 | tf_op jit(solution)/shard_map/ppermute | solution.py:27
  196.5 11.1 %collective-permute-start.1 = (bf16[1,1,32,2048]{3,2,0,1:T(8,128)(2,1)}, bf16[1,1,32,2048]{3,2,0,1:T(8,128)(2,1)}, u32[]{:S(2)}, u32[]{:S(2)}) collective-permute-start(bf16[1,1,32,2048]{3,2,0,1:T(8,128)(2,1)} %get-tuple-element.44), channel_id=1, source_target_pairs={{0,2},{1,3},{2,4},{3,5},{4,6},{5,7},{6,8},{7,9},{8,10},{9,11},{10,... | collective-permute-start | bytes 393224 | tf_op jit(solution)/shard_map/ppermute | solution.py:27
  199.2 10.0 %collective-permute-start.2 = (bf16[1,1,32,2048]{3,2,0,1:T(8,128)(2,1)}, bf16[1,1,32,2048]{3,2,0,1:T(8,128)(2,1)S(1)}, u32[]{:S(2)}, u32[]{:S(2)}) collective-permute-start(bf16[1,1,32,2048]{3,2,0,1:T(8,128)(2,1)} %get-tuple-element.43), channel_id=1, source_target_pairs={{0,3},{1,4},{2,5},{3,6},{4,7},{5,8},{6,9},{7,10},{8,11},{9,12},{10... | collective-permute-start | bytes 393224 | tf_op jit(solution)/shard_map/ppermute | solution.py:27
  200.3 11.1 %collective-permute-start.3 = (bf16[1,1,32,2048]{3,2,0,1:T(8,128)(2,1)}, bf16[1,1,32,2048]{3,2,0,1:T(8,128)(2,1)S(1)}, u32[]{:S(2)}, u32[]{:S(2)}) collective-permute-start(bf16[1,1,32,2048]{3,2,0,1:T(8,128)(2,1)} %get-tuple-element.42), channel_id=1, source_target_pairs={{0,4},{1,5},{2,6},{3,7},{4,8},{5,9},{6,10},{7,11},{8,12},{9,13},{1... | collective-permute-start | bytes 393224 | tf_op jit(solution)/shard_map/ppermute | solution.py:27
  204.5 9.4 %collective-permute-start.4 = (bf16[1,1,32,2048]{3,2,0,1:T(8,128)(2,1)}, bf16[1,1,32,2048]{3,2,0,1:T(8,128)(2,1)S(1)}, u32[]{:S(2)}, u32[]{:S(2)}) collective-permute-start(bf16[1,1,32,2048]{3,2,0,1:T(8,128)(2,1)} %get-tuple-element.41), channel_id=1, source_target_pairs={{0,5},{1,6},{2,7},{3,8},{4,9},{5,10},{6,11},{7,12},{8,13},{9,14},{... | collective-permute-start | bytes 393224 | tf_op jit(solution)/shard_map/ppermute | solution.py:27
  204.5 24.7 %collective-permute-start.5 = (bf16[1,1,32,2048]{3,2,0,1:T(8,128)(2,1)}, bf16[1,1,32,2048]{3,2,0,1:T(8,128)(2,1)S(1)}, u32[]{:S(2)}, u32[]{:S(2)}) collective-permute-start(bf16[1,1,32,2048]{3,2,0,1:T(8,128)(2,1)} %get-tuple-element.40), channel_id=1, source_target_pairs={{0,6},{1,7},{2,8},{3,9},{4,10},{5,11},{6,12},{7,13},{8,14},{9,15},... | collective-permute-start | bytes 393224 | tf_op jit(solution)/shard_map/ppermute | solution.py:27
  207.7 27.0 %collective-permute-start.6 = (bf16[1,1,32,2048]{3,2,0,1:T(8,128)(2,1)}, bf16[1,1,32,2048]{3,2,0,1:T(8,128)(2,1)S(1)}, u32[]{:S(2)}, u32[]{:S(2)}) collective-permute-start(bf16[1,1,32,2048]{3,2,0,1:T(8,128)(2,1)} %get-tuple-element.39), channel_id=1, source_target_pairs={{0,7},{1,8},{2,9},{3,10},{4,11},{5,12},{6,13},{7,14},{8,15},{9,0},... | collective-permute-start | bytes 393224 | tf_op jit(solution)/shard_map/ppermute | solution.py:27
  209.2 29.8 %collective-permute-start.7 = (bf16[1,1,32,2048]{3,2,0,1:T(8,128)(2,1)}, bf16[1,1,32,2048]{3,2,0,1:T(8,128)(2,1)S(1)}, u32[]{:S(2)}, u32[]{:S(2)}) collective-permute-start(bf16[1,1,32,2048]{3,2,0,1:T(8,128)(2,1)} %get-tuple-element.38), channel_id=1, source_target_pairs={{0,8},{1,9},{2,10},{3,11},{4,12},{5,13},{6,14},{7,15},{8,0},{9,1},... | collective-permute-start | bytes 393224 | tf_op jit(solution)/shard_map/ppermute | solution.py:27
  211.4 28.3 %collective-permute-start.8 = (bf16[1,1,32,2048]{3,2,0,1:T(8,128)(2,1)}, bf16[1,1,32,2048]{3,2,0,1:T(8,128)(2,1)S(1)}, u32[]{:S(2)}, u32[]{:S(2)}) collective-permute-start(bf16[1,1,32,2048]{3,2,0,1:T(8,128)(2,1)} %get-tuple-element.37), channel_id=1, source_target_pairs={{0,9},{1,10},{2,11},{3,12},{4,13},{5,14},{6,15},{7,0},{8,1},{9,2},... | collective-permute-start | bytes 393224 | tf_op jit(solution)/shard_map/ppermute | solution.py:27
  213.9 28.9 %collective-permute-start.9 = (bf16[1,1,32,2048]{3,2,0,1:T(8,128)(2,1)}, bf16[1,1,32,2048]{3,2,0,1:T(8,128)(2,1)S(1)}, u32[]{:S(2)}, u32[]{:S(2)}) collective-permute-start(bf16[1,1,32,2048]{3,2,0,1:T(8,128)(2,1)} %get-tuple-element.36), channel_id=1, source_target_pairs={{0,10},{1,11},{2,12},{3,13},{4,14},{5,15},{6,0},{7,1},{8,2},{9,3},... | collective-permute-start | bytes 393224 | tf_op jit(solution)/shard_map/ppermute | solution.py:27
  229.2 14.3 %collective-permute-start.10 = (bf16[1,1,32,2048]{3,2,0,1:T(8,128)(2,1)}, bf16[1,1,32,2048]{3,2,0,1:T(8,128)(2,1)S(1)}, u32[]{:S(2)}, u32[]{:S(2)}) collective-permute-start(bf16[1,1,32,2048]{3,2,0,1:T(8,128)(2,1)} %get-tuple-element.35), channel_id=1, source_target_pairs={{0,11},{1,12},{2,13},{3,14},{4,15},{5,0},{6,1},{7,2},{8,3},{9,4},{... | collective-permute-start | bytes 393224 | tf_op jit(solution)/shard_map/ppermute | solution.py:27
  234.7 10.9 %collective-permute-start.11 = (bf16[1,1,32,2048]{3,2,0,1:T(8,128)(2,1)}, bf16[1,1,32,2048]{3,2,0,1:T(8,128)(2,1)S(1)}, u32[]{:S(2)}, u32[]{:S(2)}) collective-permute-start(bf16[1,1,32,2048]{3,2,0,1:T(8,128)(2,1)} %get-tuple-element.34), channel_id=1, source_target_pairs={{0,12},{1,13},{2,14},{3,15},{4,0},{5,1},{6,2},{7,3},{8,4},{9,5},{1... | collective-permute-start | bytes 393224 | tf_op jit(solution)/shard_map/ppermute | solution.py:27
  239.0 7.2 %collective-permute-start.12 = (bf16[1,1,32,2048]{3,2,0,1:T(8,128)(2,1)S(1)}, bf16[1,1,32,2048]{3,2,0,1:T(8,128)(2,1)S(1)}, u32[]{:S(2)}, u32[]{:S(2)}) collective-permute-start(bf16[1,1,32,2048]{3,2,0,1:T(8,128)(2,1)S(1)} %get-tuple-element.33), channel_id=1, source_target_pairs={{0,13},{1,14},{2,15},{3,0},{4,1},{5,2},{6,3},{7,4},{8,5},{9,6},{10... | collective-permute-start | bytes 393224 | tf_op jit(solution)/shard_map/ppermute | solution.py:27
  239.7 10.1 %collective-permute-start.13 = (bf16[1,1,32,2048]{3,2,0,1:T(8,128)(2,1)S(1)}, bf16[1,1,32,2048]{3,2,0,1:T(8,128)(2,1)S(1)}, u32[]{:S(2)}, u32[]{:S(2)}) collective-permute-start(bf16[1,1,32,2048]{3,2,0,1:T(8,128)(2,1)S(1)} %get-tuple-element.32), channel_id=1, source_target_pairs={{0,14},{1,15},{2,0},{3,1},{4,2},{5,3},{6,4},{7,5},{8,6},{9,7},{10,... | collective-permute-start | bytes 393224 | tf_op jit(solution)/shard_map/ppermute | solution.py:27
  242.7 7.8 %collective-permute-start.14 = (bf16[1,1,32,2048]{3,2,0,1:T(8,128)(2,1)S(1)}, bf16[1,1,32,2048]{3,2,0,1:T(8,128)(2,1)S(1)}, u32[]{:S(2)}, u32[]{:S(2)}) collective-permute-start(bf16[1,1,32,2048]{3,2,0,1:T(8,128)(2,1)S(1)} %get-tuple-element.31), channel_id=1, source_target_pairs={{0,15},{1,0},{2,1},{3,2},{4,3},{5,4},{6,5},{7,6},{8,7},{9,8},{10,9... | collective-permute-start | bytes 393224 | tf_op jit(solution)/shard_map/ppermute | solution.py:27
Sparse Core Ops, SparseCore 0:
  9.6 81.6 all-gather.1
  95.1 21.3 reduce-scatter.1
